TPU v7x, 32 devices: a whole 2x2x4 slice. The times are simulated.
32 devices in a mesh: rep: 2 (over y), tract: 4 (over x, core), head: 4 (over z).
Axes of the slice: x: 2, y: 2, z: 4, core: 2. Of those that a mesh axis runs over, the one named last changes fastest.
Arguments:
- frames: bfloat16 [8, 256, 6144], P(('rep', 'tract'), 'head'), parts along dimension 0, may hold values from -7 to 7
- levels: int32 [8], P(('rep', 'tract')), parts along dimension 0, may hold values from 0 to 7
- visible: int32 [8, 4], P(('rep', 'tract')), parts along dimension 0, may hold values from 0 to 1, as said below
- w_qkv: bfloat16 [6144, 3, 1024], P(None, None, 'head'), may hold values from -0.2 to 0.2
- w_out: bfloat16 [1024, 6144], P('head'), may hold values from -1.5 to 1.5
- modulation: float32 [8, 3, 6144], replicated, may hold values from -3 to 3
Outputs:
- mixed: bfloat16 [8, 256, 6144], P(('rep', 'tract'), 'head'), parts along dimension 0
There are 2 independent parts, one for each index of `rep`. A program takes and returns all parts, laid end to end along the dimension named above; an argument that names none is the same for every part. Nothing has to cross between parts.
Inputs may be any that keep to these rules, and one draw needn't show every extreme that they name: visible[c, c] is 1 and visible[c, j] is 0 for every j > c.
All inputs are finite; a program needn't handle non-finite values.
Results may differ from a plain program's by a relative error of at most 0.019.
Values may be sent and summed in bfloat16 or wider, within the bound.
A program may use at most 64 MiB of HBM per device.

v0:
```python
import jax
import jax.numpy as jnp
from jax import lax
from jax.sharding import PartitionSpec as P

HD = 128


def from_behind(value, axis, by):
    count = lax.axis_size(axis)
    pairs = [(i, i + by) for i in range(count) if 0 <= i + by < count]
    return lax.ppermute(value, axis, pairs)


def body(frames, levels, visible, w_qkv, w_out, modulation):
    col_width = w_qkv.shape[2]
    heads_here = col_width // HD
    n_levels = modulation.shape[0]
    chosen = (lax.iota(jnp.int32, n_levels) == levels[0]).astype(jnp.float32)
    styles = jnp.tensordot(chosen, modulation, axes=1, precision=lax.Precision.HIGHEST)
    floats = lax.all_gather(frames, "head", axis=1, tiled=True).astype(jnp.float32)
    normed = floats * lax.rsqrt(jnp.mean(floats * floats, axis=-1, keepdims=True) + 1e-06)
    shaped = (normed * (1.0 + styles[1]) + styles[0]).astype(jnp.bfloat16)
    qkv = jnp.einsum("crd,dke->crke", shaped, w_qkv, preferred_element_type=jnp.float32).astype(
        jnp.bfloat16
    )
    total_rows = qkv.shape[1]
    queries = qkv[0, :, 0].reshape(total_rows, heads_here, HD)
    kv_block = qkv[:, :, 1:]
    visible_row = visible[0]
    score_scale = HD ** (-0.5)

    def absorb(state, incoming, offset):
        row_peak, denominator, running = state
        blocks = incoming.shape[0]
        allowed = (lax.dynamic_slice_in_dim(visible_row, offset, blocks) > 0) & (offset >= 0)
        key_rows = incoming[:, :, 0].reshape(blocks, total_rows, heads_here, HD)
        values = incoming[:, :, 1].reshape(blocks, total_rows, heads_here, HD)
        scores = (
            jnp.einsum("qhd,nkhd->qhnk", queries, key_rows, preferred_element_type=jnp.float32)
            * score_scale
        )
        allowed = allowed[None, None, :, None]
        scores = jnp.where(allowed, scores, -1e30)
        new_peak = jnp.maximum(row_peak, jnp.max(scores, axis=(2, 3)))
        probs = jnp.where(allowed, jnp.exp(scores - new_peak[:, :, None, None]), 0.0)
        rescale = jnp.exp(row_peak - new_peak)
        denominator = denominator * rescale + jnp.sum(probs, axis=(2, 3))
        weighted = jnp.einsum(
            "qhnk,nkhd->qhd", probs.astype(jnp.bfloat16), values, preferred_element_type=jnp.float32
        )
        running = running * rescale[:, :, None] + weighted
        return (new_peak, denominator, running)

    initial = (
        jnp.full((total_rows, heads_here), -1e30, jnp.float32),
        jnp.zeros((total_rows, heads_here), jnp.float32),
        jnp.zeros((total_rows, heads_here, HD), jnp.float32),
    )
    own_index = lax.axis_index("tract")
    state = absorb(initial, kv_block, own_index)
    for distance in range(1, lax.axis_size("tract")):
        moved = from_behind(kv_block, "tract", distance)
        state = absorb(state, moved, own_index - distance)
    row_peak, denominator, running = state
    attended = (
        (running / denominator[:, :, None]).astype(jnp.bfloat16).reshape(total_rows, col_width)
    )
    summed = lax.psum_scatter(
        jnp.dot(attended, w_out, preferred_element_type=jnp.float32).astype(jnp.bfloat16),
        "head",
        scatter_dimension=0,
        tiled=True,
    ).astype(jnp.float32)
    mixed = (summed * styles[2]).astype(jnp.bfloat16)
    return mixed[None]


def solution(mesh):
    placed = (
        P(("rep", "tract"), "head", None),
        P(("rep", "tract")),
        P(("rep", "tract"), None),
        P(None, None, "head"),
        P("head", None),
        P(),
    )
    return jax.shard_map(
        body,
        mesh=mesh,
        in_specs=placed,
        out_specs=P(("rep", "tract"), "head", None),
        check_vma=False,
    )
```

profile of v0, /device:TPU:10, one launch (start us, length us, event | category | flops | bytes accessed | tf_op | source)
XLA Modules:
  0.0 173.0 jit_solution(12812611216690335462)
XLA Ops:
  6.5 0.7 all-gather.2.cloned.1.call-update
  8.1 1.5 constant_dynamic-slice_fusion.2
  12.1 1.5 fusion.62
  13.7 57.7 %all-gather.2.cloned.1.call-done = bf16[1,256,6144]{2,1,0:T(8,128)(2,1)} async-done(((bf16[1,64,6144]{2,1,0:T(8,128)(2,1)}), bf16[1,256,6144]{2,1,0:T(8,128)(2,1)}) %all-gather.2.cloned.1.call-update) | async-done | bytes 3145744 | tf_op jit(solution)/shard_map/all_gather | solution.py:21
  71.3 2.7 %fusion = f32[256]{0:T(256)S(1)} fusion(bf16[1,256,6144]{2,1,0:T(8,128)(2,1)} %all-gather.2.cloned.1.call-done), kind=kLoop, calls=%fused_computation.3 | loop fusion | flops 4718336 | bytes 3146752 | tf_op jit(solution)/shard_map/reduce_sum | solution.py:22
  74.2 7.8 %fusion.21 = bf16[1,256,3,256]{1,3,2,0:T(8,128)(2,1)S(1)} fusion(bf16[6144,3,256]{2,0,1:T(8,128)(2,1)} %param.9, bf16[1,256,6144]{2,1,0:T(8,128)(2,1)S(1)} %copy-done.1, f32[6144]{0:T(1024)S(1)} %bitcast.130, f32[6144]{0:T(1024)S(1)} %bitcast.131, f32[256]{0:T(256)S(1)} %add_rsqrt_fusion), kind=kOutput, calls=%fused_computation.26 | convolution fusion | flops 2423980032 | bytes 13026304 | tf_op jit(solution)/shard_map/crd,dke->crke/dot_general | solution.py:24
  82.0 0.7 collective-permute-start.2
  82.7 1.3 collective-permute-start.1
  84.0 2.0 %collective-permute-start = (bf16[1,256,2,256]{1,3,2,0:T(8,128)(2,1)S(1)}, bf16[1,256,2,256]{1,3,2,0:T(8,128)(2,1)S(1)}, u32[]{:S(2)}, u32[]{:S(2)}) collective-permute-start(bf16[1,256,2,256]{1,3,2,0:T(8,128)(2,1)S(1)} %slice.59), channel_id=1, source_target_pairs={{0,4},{4,8},{8,12},{1,5},{5,9},{9,13},{2,6},{6,10},{10,14},{3,7},{... | collective-permute-start | bytes 786440 | tf_op jit(solution)/shard_map/ppermute | solution.py:12
  86.1 0.3 fusion.82
  86.4 10.7 %collective-permute-done.1 = bf16[1,256,2,256]{1,3,2,0:T(8,128)(2,1)S(1)} collective-permute-done((bf16[1,256,2,256]{1,3,2,0:T(8,128)(2,1)S(1)}, bf16[1,256,2,256]{1,3,2,0:T(8,128)(2,1)S(1)}, u32[]{:S(2)}, u32[]{:S(2)}) %collective-permute-start.1) | collective-permute-done | bytes 262176 | tf_op jit(solution)/shard_map/ppermute | solution.py:12
  97.1 0.7 collective-permute-done
  97.8 0.3 fusion.81
  98.1 0.3 fusion.80
  98.5 0.3 fusion.79
  98.8 0.2 fusion.34
  99.0 0.2 fusion.38
  99.2 0.2 fusion.31
  99.4 0.2 fusion.29
  99.7 0.2 fusion.27
  99.9 0.2 fusion.32
  100.2 2.7 %convolution_convert_fusion = bf16[256,6144]{1,0:T(8,128)(2,1)} fusion(bf16[256,256]{0,1:T(8,128)(2,1)S(1)} %bitcast.127, bf16[256,6144]{1,0:T(8,128)(2,1)S(1)} %copy-done), kind=kOutput, calls=%fused_computation.2 | convolution fusion | flops 806879232 | bytes 6422528 | tf_op jit(solution)/shard_map/dot_general | solution.py:70
  102.9 61.1 %reduce-scatter.2.cloned.1.call-done = bf16[64,6144]{1,0:T(8,128)(2,1)} async-done(((bf16[256,6144]{1,0:T(8,128)(2,1)}), bf16[64,6144]{1,0:T(8,128)(2,1)}) %reduce-scatter.2.cloned.1.call-update) | async-done | bytes 786448 | tf_op jit(solution)/shard_map/reduce_scatter | solution.py:69
  164.0 2.2 %fusion.33 = bf16[1,64,6144]{2,1,0:T(8,128)(2,1)} fusion(bf16[64,6144]{1,0:T(8,128)(2,1)} %reduce-scatter.2.cloned.1.call-done, f32[6144]{0:T(1024)S(1)} %bitcast.129), kind=kLoop, calls=%fused_computation.40 | loop fusion | flops 1179648 | bytes 1597440 | tf_op jit(solution)/shard_map/broadcast_in_dim | solution.py:76
  (18 shorter events, 0.4 us)
Async XLA Ops:
  6.5 93.6 %copy-start = (bf16[256,6144]{1,0:T(8,128)(2,1)S(1)}, bf16[256,6144]{1,0:T(8,128)(2,1)}, u32[]{:S(2)}) copy-start(bf16[256,6144]{1,0:T(8,128)(2,1)} %param.10) | copy-start | bytes 9437188
  6.5 64.8 %all-gather.2.cloned.1.call-start = ((), (), s32[]{:S(2)}) async-start(), calls=%async_computation.1 | async-start | bytes 3932160 | tf_op jit(solution)/shard_map/all_gather | solution.py:21
  7.3 156.8 %reduce-scatter.2.cloned.1.call-start = ((), (), s32[]{:S(2)}) async-start(), calls=%async_computation.2 | async-start | bytes 3932160 | tf_op jit(solution)/shard_map/reduce_scatter | solution.py:69
  71.3 2.8 %copy-start.1 = (bf16[1,256,6144]{2,1,0:T(8,128)(2,1)S(1)}, bf16[1,256,6144]{2,1,0:T(8,128)(2,1)}, u32[]{:S(2)}) copy-start(bf16[1,256,6144]{2,1,0:T(8,128)(2,1)} %all-gather.2.cloned.1.call-done) | copy-start | bytes 9437188
  82.0 16.4 %collective-permute-start.2 = (bf16[1,256,2,256]{1,3,2,0:T(8,128)(2,1)S(1)}, bf16[1,256,2,256]{1,3,2,0:T(8,128)(2,1)S(1)}, u32[]{:S(2)}, u32[]{:S(2)}) collective-permute-start(bf16[1,256,2,256]{1,3,2,0:T(8,128)(2,1)S(1)} %slice.59), channel_id=1, source_target_pairs={{0,12},{1,13},{2,14},{3,15},{16,28},{17,29},{18,30},{19,31}} | collective-permute-start | bytes 786440 | tf_op jit(solution)/shard_map/ppermute | solution.py:12
  82.7 14.4 %collective-permute-start.1 = (bf16[1,256,2,256]{1,3,2,0:T(8,128)(2,1)S(1)}, bf16[1,256,2,256]{1,3,2,0:T(8,128)(2,1)S(1)}, u32[]{:S(2)}, u32[]{:S(2)}) collective-permute-start(bf16[1,256,2,256]{1,3,2,0:T(8,128)(2,1)S(1)} %slice.59), channel_id=1, source_target_pairs={{0,8},{4,12},{1,9},{5,13},{2,10},{6,14},{3,11},{7,15},{16,24},{20,... | collective-permute-start | bytes 786440 | tf_op jit(solution)/shard_map/ppermute | solution.py:12
  84.0 13.8 %collective-permute-start = (bf16[1,256,2,256]{1,3,2,0:T(8,128)(2,1)S(1)}, bf16[1,256,2,256]{1,3,2,0:T(8,128)(2,1)S(1)}, u32[]{:S(2)}, u32[]{:S(2)}) collective-permute-start(bf16[1,256,2,256]{1,3,2,0:T(8,128)(2,1)S(1)} %slice.59), channel_id=1, source_target_pairs={{0,4},{4,8},{8,12},{1,5},{5,9},{9,13},{2,6},{6,10},{10,14},{3,7},{... | collective-permute-start | bytes 786440 | tf_op jit(solution)/shard_map/ppermute | solution.py:12
Sparse Core Ops, SparseCore 0:
  8.9 62.3 all-gather.1
  103.0 60.9 reduce-scatter.1
where the time goes:
time: 176 us; the launch traced here: 173 us
  waiting for transfers between devices  131 us (74%)
  between operations  16.9 us (10%)
  matrix products  14 us (8%)
  other arithmetic  5.39 us (3%)
  starting transfers between devices  4.04 us (2%)
    reduce_scatter x1, waiting for transfers between devices, body(): lax.psum_scatter(jnp.dot(attended, w_out, preferred_element_type=jnp.floa...  61.1 us
    all_gather x1, waiting for transfers between devices, body(): lax.all_gather(frames, 'head', axis=1, tiled=True).astype(jnp.float32)  57.7 us
    ppermute x3, waiting for transfers between devices, from_behind(): return lax.ppermute(value, axis, pairs)  11.4 us
    dot_general x1, matrix products, body(): jnp.einsum('crd,dke->crke', shaped, w_qkv, preferred_element_type=jnp.flo...  7.82 us
    ppermute x3, starting transfers between devices, from_behind(): return lax.ppermute(value, axis, pairs)  4 us
  transfers between devices with their start and end apart: 5, of which 4 were waited for; matrix products, arithmetic and copies ran while one was open for 2% of the time, Pallas kernels for 0%

commit v1 on v0

--- a/solution.py
+++ b/solution.py
@@ -1,9 +1,215 @@
+import functools
+
 import jax
 import jax.numpy as jnp
 from jax import lax
+from jax.experimental import pallas as pl
+from jax.experimental.pallas import tpu as pltpu
 from jax.sharding import PartitionSpec as P
 
 HD = 128
+MESH = pl.DeviceIdType.MESH
+
+
+def meet(n, me):
+    barrier = pltpu.get_barrier_semaphore()
+    for other in (lax.rem(me + 1, n), lax.rem(me + n - 1, n)):
+        pl.semaphore_signal(barrier, inc=1, device_id={"head": other}, device_id_type=MESH)
+    pl.semaphore_wait(barrier, 2)
+
+
+def gather_kernel(n, pieces, x_ref, out_ref, send_sem, recv_sem):
+    me = lax.axis_index("head")
+    meet(n, me)
+    rows = x_ref.shape[1]
+    step_rows = rows // pieces
+
+    def copy(way, step, piece):
+        block = me - way * step
+        span = pl.ds(piece * step_rows, step_rows)
+        return pltpu.make_async_remote_copy(
+            src_ref=(x_ref.at[0] if step == 0 else out_ref.at[block]).at[span],
+            dst_ref=out_ref.at[block].at[span],
+            send_sem=send_sem.at[(way + 1) // 2, step, piece],
+            recv_sem=recv_sem.at[(way + 1) // 2, step, piece],
+            device_id={"head": me + way},
+            device_id_type=MESH,
+        )
+
+    def arrival(way, step, piece):
+        block = me - way * (step + 1)
+        span = pl.ds(piece * step_rows, step_rows)
+        return pltpu.make_async_remote_copy(
+            src_ref=x_ref.at[0].at[span],
+            dst_ref=out_ref.at[block].at[span],
+            send_sem=send_sem.at[(way + 1) // 2, step, piece],
+            recv_sem=recv_sem.at[(way + 1) // 2, step, piece],
+            device_id={"head": me - way},
+            device_id_type=MESH,
+        )
+
+    def sends(way, step):
+        block, target = me - way * step, me + way
+        return (block >= 0) & (block < n) & (target >= 0) & (target < n)
+
+    def receives(way, step):
+        block = me - way * (step + 1)
+        return (block >= 0) & (block < n)
+
+    for piece in range(pieces):
+        for way in (-1, 1):
+
+            @pl.when(sends(way, 0))
+            def _():
+                copy(way, 0, piece).start()
+
+    out_ref[me] = x_ref[0]
+    for step in range(n - 1):
+        for piece in range(pieces):
+            for way in (-1, 1):
+
+                @pl.when(receives(way, step))
+                def _():
+                    arrival(way, step, piece).wait_recv()
+
+                if step < n - 2:
+
+                    @pl.when(sends(way, step + 1))
+                    def _():
+                        copy(way, step + 1, piece).start()
+
+    for step in range(n - 1):
+        for piece in range(pieces):
+            for way in (-1, 1):
+
+                @pl.when(sends(way, step))
+                def _():
+                    copy(way, step, piece).wait_send()
+
+
+def gather_rows(frames, n):
+    rows, width = frames.shape[1:]
+    pieces = max(1, rows // 32)
+    return pl.pallas_call(
+        functools.partial(gather_kernel, n, pieces),
+        out_shape=jax.ShapeDtypeStruct((n, rows, width), frames.dtype),
+        in_specs=[pl.BlockSpec(memory_space=pltpu.VMEM)],
+        out_specs=pl.BlockSpec(memory_space=pltpu.VMEM),
+        scratch_shapes=[
+            pltpu.SemaphoreType.DMA((2, n, pieces)),
+            pltpu.SemaphoreType.DMA((2, n, pieces)),
+        ],
+        compiler_params=pltpu.CompilerParams(
+            collective_id=0, has_side_effects=True, vmem_limit_bytes=24 << 20
+        ),
+    )(frames)
+
+
+def scatter_kernel(n, pieces, a_ref, w_ref, out_ref, going, landed, send_sem, recv_sem):
+    me = lax.axis_index("head")
+    meet(n, me)
+    rows = out_ref.shape[0]
+    width = w_ref.shape[1]
+    cols = width // pieces
+
+    def copy(way, step, piece):
+        side = (way + 1) // 2
+        span = pl.ds(piece * cols, cols)
+        return pltpu.make_async_remote_copy(
+            src_ref=going.at[side, step].at[:, span],
+            dst_ref=landed.at[side, step].at[:, span],
+            send_sem=send_sem.at[side, step, piece],
+            recv_sem=recv_sem.at[side, step, piece],
+            device_id={"head": me + way},
+            device_id_type=MESH,
+        )
+
+    def product(block, piece):
+        return jnp.dot(
+            a_ref[block],
+            w_ref[:, piece * cols : (piece + 1) * cols],
+            preferred_element_type=jnp.float32,
+        )
+
+    def owner(way, step):
+        return (n - 1 - step) if way == 1 else step
+
+    def sends(way, step):
+        block = owner(way, step)
+        return block > me if way == 1 else block < me
+
+    def receives(way, step):
+        block = owner(way, step)
+        return (block >= me) & (me > 0) if way == 1 else (block <= me) & (me < n - 1)
+
+    @pl.loop(0, n - 1)
+    def _(tick):
+        for piece in range(pieces):
+            span = slice(piece * cols, (piece + 1) * cols)
+            for way in (-1, 1):
+                side = (way + 1) // 2
+                step = tick - (me if way == 1 else n - 1 - me)
+                held = (step >= 0) & (step < n - 1)
+
+                @pl.when(held & sends(way, step))
+                def _():
+                    going[side, step, :, span] = product(owner(way, step), piece).astype(
+                        going.dtype
+                    )
+
+                    @pl.when(receives(way, step))
+                    def _():
+                        copy(way, step, piece).wait_recv()
+                        going[side, step, :, span] = (
+                            going[side, step, :, span].astype(jnp.float32)
+                            + landed[side, step, :, span].astype(jnp.float32)
+                        ).astype(going.dtype)
+
+                    copy(way, step, piece).start()
+
+    for piece in range(pieces):
+        span = slice(piece * cols, (piece + 1) * cols)
+        out_ref[:, span] = product(me, piece).astype(going.dtype).astype(jnp.float32)
+    for piece in range(pieces):
+        span = slice(piece * cols, (piece + 1) * cols)
+        for way in (-1, 1):
+            side = (way + 1) // 2
+            last = n - 1 - me if way == 1 else me
+
+            @pl.when(last < n - 1)
+            def _():
+                copy(way, last, piece).wait_recv()
+                out_ref[:, span] += landed[side, last, :, span].astype(jnp.float32)
+
+    @pl.loop(0, n - 1)
+    def _(step):
+        for piece in range(pieces):
+            for way in (-1, 1):
+
+                @pl.when(sends(way, step))
+                def _():
+                    copy(way, step, piece).wait_send()
+
+
+def scatter_sum(attended, w_out, n):
+    total, depth = attended.shape
+    rows, width = total // n, w_out.shape[1]
+    pieces = 2 if rows >= 64 else 1
+    return pl.pallas_call(
+        functools.partial(scatter_kernel, n, pieces),
+        out_shape=jax.ShapeDtypeStruct((rows, width), jnp.float32),
+        in_specs=[pl.BlockSpec(memory_space=pltpu.VMEM)] * 2,
+        out_specs=pl.BlockSpec(memory_space=pltpu.VMEM),
+        scratch_shapes=[
+            pltpu.VMEM((2, n - 1, rows, width), jnp.bfloat16),
+            pltpu.VMEM((2, n - 1, rows, width), jnp.bfloat16),
+            pltpu.SemaphoreType.DMA((2, n, pieces)),
+            pltpu.SemaphoreType.DMA((2, n, pieces)),
+        ],
+        compiler_params=pltpu.CompilerParams(
+            collective_id=1, has_side_effects=True, vmem_limit_bytes=40 << 20
+        ),
+    )(attended.reshape(n, rows, depth), w_out)
 
 
 def from_behind(value, axis, by):
@@ -18,7 +224,8 @@
     n_levels = modulation.shape[0]
     chosen = (lax.iota(jnp.int32, n_levels) == levels[0]).astype(jnp.float32)
     styles = jnp.tensordot(chosen, modulation, axes=1, precision=lax.Precision.HIGHEST)
-    floats = lax.all_gather(frames, "head", axis=1, tiled=True).astype(jnp.float32)
+    ranks = lax.axis_size("head")
+    floats = gather_rows(frames, ranks).reshape(1, -1, frames.shape[2]).astype(jnp.float32)
     normed = floats * lax.rsqrt(jnp.mean(floats * floats, axis=-1, keepdims=True) + 1e-06)
     shaped = (normed * (1.0 + styles[1]) + styles[0]).astype(jnp.bfloat16)
     qkv = jnp.einsum("crd,dke->crke", shaped, w_qkv, preferred_element_type=jnp.float32).astype(
@@ -66,12 +273,7 @@
     attended = (
         (running / denominator[:, :, None]).astype(jnp.bfloat16).reshape(total_rows, col_width)
     )
-    summed = lax.psum_scatter(
-        jnp.dot(attended, w_out, preferred_element_type=jnp.float32).astype(jnp.bfloat16),
-        "head",
-        scatter_dimension=0,
-        tiled=True,
-    ).astype(jnp.float32)
+    summed = scatter_sum(attended, w_out, ranks)
     mixed = (summed * styles[2]).astype(jnp.bfloat16)
     return mixed[None]
 

time: 176 us -> 145 us (0.82)
  the two profiles are of different devices: /device:TPU:10 before, /device:TPU:0 now
where the time goes in v1:
time: 145 us
  Pallas kernels  110 us (76%)
  matrix products  10 us (7%)
  local copies, waits for them, and re-layouts  6.15 us (4%)
  starting transfers between devices  5.39 us (4%)
  other arithmetic  5.13 us (4%)
  waiting for transfers between devices  4.52 us (3%)
  between operations  3.54 us (2%)
    pallas_call x1, Pallas kernels, gather_rows(): pl.pallas_call(functools.partial(gather_kernel, n, pieces), out_shape=jax...  55.9 us
    pallas_call x1, Pallas kernels, scatter_sum(): pl.pallas_call(functools.partial(scatter_kernel, n, pieces), out_shape=ja...  54.1 us
    dot_general x1, matrix products, body(): jnp.einsum('crd,dke->crke', shaped, w_qkv, preferred_element_type=jnp.flo...  7.57 us
    ppermute x3, starting transfers between devices, from_behind(): return lax.ppermute(value, axis, pairs)  5.39 us
    unnamed x10, local copies, waits for them, and re-layouts  5.04 us
    ppermute x3, waiting for transfers between devices, from_behind(): return lax.ppermute(value, axis, pairs)  4.52 us
    convert_element_type x1, other arithmetic, body(): shaped = (normed * (1.0 + styles[1]) + styles[0]).astype(jnp.bfloat16)  2.94 us
  transfers between devices with their start and end apart: 3, of which 1 were waited for; matrix products, arithmetic and copies ran while one was open for 1% of the time, Pallas kernels for 0%

profile of v1, /device:TPU:0, one launch (start us, length us, event | category | flops | bytes accessed | tf_op | source)
XLA Modules:
  0.0 144.7 jit_solution(8463529446727328776)
XLA Ops:
  0.7 0.4 copy-done
  1.1 0.4 fusion.57
  1.6 1.1 copy-done.3
  2.7 55.9 %shard_map.64 = bf16[4,64,6144]{2,1,0:T(8,128)(2,1)S(1)} custom-call(bf16[1,64,6144]{2,1,0:T(8,128)(2,1)S(1)} %copy-done.3), custom_call_target="tpu_custom_call" | custom-call | tf_op jit(solution)/shard_map/pallas_call | solution.py:93
  58.6 1.7 %copy-done.1 = bf16[4,64,6144]{2,1,0:T(8,128)(2,1)} copy-done((bf16[4,64,6144]{2,1,0:T(8,128)(2,1)}, bf16[4,64,6144]{2,1,0:T(8,128)(2,1)S(1)}, u32[]{:S(2)}) %copy-start.1) | copy-done | bytes 3145752
  60.3 0.7 multiply_reduce_fusion
  61.1 2.9 %fusion.2 = bf16[256,6144]{1,0:T(8,128)(2,1)S(1)} fusion(f32[6144]{0:T(1024)S(1)} %bitcast.133, f32[6144]{0:T(1024)S(1)} %bitcast.134, f32[256]{0:T(256)S(1)} %rsqrt.12, bf16[4,64,6144]{2,1,0:T(8,128)(2,1)} %copy-done.1), kind=kLoop, calls=%fused_computation.3 | loop fusion | flops 7864320 | bytes 6341632 | tf_op jit(solution)/shard_map/convert_element_type | solution.py:230
  64.0 7.6 %fusion.16 = bf16[1,256,3,256]{1,3,2,0:T(8,128)(2,1)S(1)} fusion(bf16[6144,3,256]{2,0,1:T(8,128)(2,1)} %param.9, bf16[256,6144]{1,0:T(8,128)(2,1)S(1)} %fusion.2), kind=kOutput, calls=%fused_computation.21 | convolution fusion | flops 2416115712 | bytes 12976128 | tf_op jit(solution)/shard_map/crd,dke->crke/dot_general | solution.py:231
  71.6 2.0 %collective-permute-start.2 = (bf16[1,256,2,256]{1,3,2,0:T(8,128)(2,1)S(1)}, bf16[1,256,2,256]{1,3,2,0:T(8,128)(2,1)S(1)}, u32[]{:S(2)}, u32[]{:S(2)}) collective-permute-start(bf16[1,256,2,256]{1,3,2,0:T(8,128)(2,1)S(1)} %slice.62), channel_id=1, source_target_pairs={{0,12},{1,13},{2,14},{3,15},{16,28},{17,29},{18,30},{19,31}} | collective-permute-start | bytes 786440 | tf_op jit(solution)/shard_map/ppermute | solution.py:218
  73.6 2.1 %collective-permute-start.1 = (bf16[1,256,2,256]{1,3,2,0:T(8,128)(2,1)S(1)}, bf16[1,256,2,256]{1,3,2,0:T(8,128)(2,1)S(1)}, u32[]{:S(2)}, u32[]{:S(2)}) collective-permute-start(bf16[1,256,2,256]{1,3,2,0:T(8,128)(2,1)S(1)} %slice.62), channel_id=1, source_target_pairs={{0,8},{4,12},{1,9},{5,13},{2,10},{6,14},{3,11},{7,15},{16,24},{20,... | collective-permute-start | bytes 786440 | tf_op jit(solution)/shard_map/ppermute | solution.py:218
  75.7 1.3 collective-permute-start
  77.1 0.7 constant_dynamic-slice_fusion.2
  78.5 0.3 fusion.77
  80.7 4.5 %collective-permute-done.1 = bf16[1,256,2,256]{1,3,2,0:T(8,128)(2,1)S(1)} collective-permute-done((bf16[1,256,2,256]{1,3,2,0:T(8,128)(2,1)S(1)}, bf16[1,256,2,256]{1,3,2,0:T(8,128)(2,1)S(1)}, u32[]{:S(2)}, u32[]{:S(2)}) %collective-permute-start.1) | collective-permute-done | bytes 262176 | tf_op jit(solution)/shard_map/ppermute | solution.py:218
  85.2 0.3 fusion.74
  85.5 0.3 fusion.75
  85.8 0.3 fusion.76
  86.6 0.2 fusion.26
  86.8 0.2 fusion.24
  87.0 0.2 fusion.22
  87.3 0.2 fusion.27
  87.8 1.9 %copy-done.2 = bf16[256,6144]{1,0:T(8,128)(2,1)S(1)} copy-done((bf16[256,6144]{1,0:T(8,128)(2,1)S(1)}, bf16[256,6144]{1,0:T(8,128)(2,1)}, u32[]{:S(2)}) %copy-start.2) | copy-done | bytes 3145752
  89.7 54.1 %shard_map.65 = f32[64,6144]{1,0:T(8,128)S(1)} custom-call(bf16[4,64,256]{2,1,0:T(8,128)(2,1)S(1)} %reshape_reshape.3.a_ref, bf16[256,6144]{1,0:T(8,128)(2,1)S(1)} %copy-done.2), custom_call_target="tpu_custom_call" | custom-call | tf_op jit(solution)/shard_map/pallas_call | solution.py:198
  143.7 1.0 fusion.28
  (23 shorter events, 1.0 us)
Async XLA Ops:
  0.0 1.1 copy-start
  1.6 1.1 copy-start.3
  58.6 1.7 %copy-start.1 = (bf16[4,64,6144]{2,1,0:T(8,128)(2,1)}, bf16[4,64,6144]{2,1,0:T(8,128)(2,1)S(1)}, u32[]{:S(2)}) copy-start(bf16[4,64,6144]{2,1,0:T(8,128)(2,1)S(1)} %shard_map.64) | copy-start | bytes 9437188
  64.0 13.0 %copy-start.4 = (s32[1,4]{1,0:T(1,128)S(1)}, s32[1,4]{1,0:T(1,128)}, u32[]{:S(2)}) copy-start(s32[1,4]{1,0:T(1,128)} %param.8) | copy-start | bytes 52
  71.6 9.0 %collective-permute-start.2 = (bf16[1,256,2,256]{1,3,2,0:T(8,128)(2,1)S(1)}, bf16[1,256,2,256]{1,3,2,0:T(8,128)(2,1)S(1)}, u32[]{:S(2)}, u32[]{:S(2)}) collective-permute-start(bf16[1,256,2,256]{1,3,2,0:T(8,128)(2,1)S(1)} %slice.62), channel_id=1, source_target_pairs={{0,12},{1,13},{2,14},{3,15},{16,28},{17,29},{18,30},{19,31}} | collective-permute-start | bytes 786440 | tf_op jit(solution)/shard_map/ppermute | solution.py:218
  73.6 11.6 %collective-permute-start.1 = (bf16[1,256,2,256]{1,3,2,0:T(8,128)(2,1)S(1)}, bf16[1,256,2,256]{1,3,2,0:T(8,128)(2,1)S(1)}, u32[]{:S(2)}, u32[]{:S(2)}) collective-permute-start(bf16[1,256,2,256]{1,3,2,0:T(8,128)(2,1)S(1)} %slice.62), channel_id=1, source_target_pairs={{0,8},{4,12},{1,9},{5,13},{2,10},{6,14},{3,11},{7,15},{16,24},{20,... | collective-permute-start | bytes 786440 | tf_op jit(solution)/shard_map/ppermute | solution.py:218
  75.7 10.1 %collective-permute-start = (bf16[1,256,2,256]{1,3,2,0:T(8,128)(2,1)S(1)}, bf16[1,256,2,256]{1,3,2,0:T(8,128)(2,1)S(1)}, u32[]{:S(2)}, u32[]{:S(2)}) collective-permute-start(bf16[1,256,2,256]{1,3,2,0:T(8,128)(2,1)S(1)} %slice.62), channel_id=1, source_target_pairs={{0,4},{4,8},{8,12},{1,5},{5,9},{9,13},{2,6},{6,10},{10,14},{3,7},{... | collective-permute-start | bytes 786440 | tf_op jit(solution)/shard_map/ppermute | solution.py:218
  87.8 1.9 %copy-start.2 = (bf16[256,6144]{1,0:T(8,128)(2,1)S(1)}, bf16[256,6144]{1,0:T(8,128)(2,1)}, u32[]{:S(2)}) copy-start(bf16[256,6144]{1,0:T(8,128)(2,1)} %w_ref.1) | copy-start | bytes 9437188

commit v2 on v1

--- a/solution.py
+++ b/solution.py
@@ -18,53 +18,75 @@
     pl.semaphore_wait(barrier, 2)
 
 
-def gather_kernel(n, pieces, x_ref, out_ref, send_sem, recv_sem):
+def project_kernel(
+    n, pieces, x_ref, style_ref, w_hbm, q_ref, kv_ref, got, w_ref, w_sem, send_sem, recv_sem
+):
     me = lax.axis_index("head")
+    load = pltpu.make_async_copy(w_hbm, w_ref, w_sem)
+    load.start()
     meet(n, me)
-    rows = x_ref.shape[1]
-    step_rows = rows // pieces
-
-    def copy(way, step, piece):
+    rows, width = x_ref.shape[1:]
+    part = rows // pieces
+
+    def copy(way, step, piece, first=False):
+        side = (way + 1) // 2
+        span = pl.ds(piece * part, part)
         block = me - way * step
-        span = pl.ds(piece * step_rows, step_rows)
         return pltpu.make_async_remote_copy(
-            src_ref=(x_ref.at[0] if step == 0 else out_ref.at[block]).at[span],
-            dst_ref=out_ref.at[block].at[span],
-            send_sem=send_sem.at[(way + 1) // 2, step, piece],
-            recv_sem=recv_sem.at[(way + 1) // 2, step, piece],
+            src_ref=(x_ref.at[0] if first else got.at[block]).at[span],
+            dst_ref=got.at[block].at[span],
+            send_sem=send_sem.at[side, step, piece],
+            recv_sem=recv_sem.at[side, step, piece],
             device_id={"head": me + way},
             device_id_type=MESH,
         )
 
     def arrival(way, step, piece):
-        block = me - way * (step + 1)
-        span = pl.ds(piece * step_rows, step_rows)
+        side = (way + 1) // 2
+        span = pl.ds(piece * part, part)
         return pltpu.make_async_remote_copy(
             src_ref=x_ref.at[0].at[span],
-            dst_ref=out_ref.at[block].at[span],
-            send_sem=send_sem.at[(way + 1) // 2, step, piece],
-            recv_sem=recv_sem.at[(way + 1) // 2, step, piece],
+            dst_ref=got.at[me - way * (step + 1)].at[span],
+            send_sem=send_sem.at[side, step, piece],
+            recv_sem=recv_sem.at[side, step, piece],
             device_id={"head": me - way},
             device_id_type=MESH,
         )
 
     def sends(way, step):
         block, target = me - way * step, me + way
-        return (block >= 0) & (block < n) & (target >= 0) & (target < n)
+        return (block >= 0) & (block < n) & (target >= 0) & (target < n) & (step < n - 1)
 
     def receives(way, step):
         block = me - way * (step + 1)
         return (block >= 0) & (block < n)
 
+    def project(block):
+        tokens = got[block].astype(jnp.float32)
+        power = jnp.mean(tokens * tokens, axis=-1, keepdims=True)
+        normed = tokens * lax.rsqrt(power + 1e-06)
+        shaped = (normed * (1.0 + style_ref[1:2, :]) + style_ref[0:1, :]).astype(jnp.bfloat16)
+        for kind in range(3):
+            made = jnp.dot(shaped, w_ref[kind], preferred_element_type=jnp.float32)
+            made = made.astype(jnp.bfloat16)
+            if kind == 0:
+                q_ref[block] = made
+            else:
+                kv_ref[kind - 1, block] = made
+
     for piece in range(pieces):
         for way in (-1, 1):
 
             @pl.when(sends(way, 0))
             def _():
-                copy(way, 0, piece).start()
-
-    out_ref[me] = x_ref[0]
-    for step in range(n - 1):
+                copy(way, 0, piece, True).start()
+
+    got[me] = x_ref[0]
+    load.wait()
+    project(me)
+
+    @pl.loop(0, n - 1)
+    def _(step):
         for piece in range(pieces):
             for way in (-1, 1):
 
@@ -72,13 +94,20 @@
                 def _():
                     arrival(way, step, piece).wait_recv()
 
-                if step < n - 2:
-
-                    @pl.when(sends(way, step + 1))
-                    def _():
-                        copy(way, step + 1, piece).start()
-
-    for step in range(n - 1):
+                @pl.when(sends(way, step + 1))
+                def _():
+                    copy(way, step + 1, piece).start()
+
+        @pl.loop(0, 2)
+        def _(side):
+            way = 2 * side - 1
+
+            @pl.when(receives(way, step))
+            def _():
+                project(me - way * (step + 1))
+
+    @pl.loop(0, n - 1)
+    def _(step):
         for piece in range(pieces):
             for way in (-1, 1):
 
@@ -87,22 +116,30 @@
                     copy(way, step, piece).wait_send()
 
 
-def gather_rows(frames, n):
+def project_rows(frames, styles, w_qkv, n):
     rows, width = frames.shape[1:]
+    cols = w_qkv.shape[2]
     pieces = max(1, rows // 32)
+    vmem = pl.BlockSpec(memory_space=pltpu.VMEM)
     return pl.pallas_call(
-        functools.partial(gather_kernel, n, pieces),
-        out_shape=jax.ShapeDtypeStruct((n, rows, width), frames.dtype),
-        in_specs=[pl.BlockSpec(memory_space=pltpu.VMEM)],
-        out_specs=pl.BlockSpec(memory_space=pltpu.VMEM),
+        functools.partial(project_kernel, n, pieces),
+        out_shape=(
+            jax.ShapeDtypeStruct((n, rows, cols), frames.dtype),
+            jax.ShapeDtypeStruct((2, n, rows, cols), frames.dtype),
+        ),
+        in_specs=[vmem, vmem, pl.BlockSpec(memory_space=pl.ANY)],
+        out_specs=(vmem, vmem),
         scratch_shapes=[
+            pltpu.VMEM((n, rows, width), frames.dtype),
+            pltpu.VMEM((3, width, cols), w_qkv.dtype),
+            pltpu.SemaphoreType.DMA,
             pltpu.SemaphoreType.DMA((2, n, pieces)),
             pltpu.SemaphoreType.DMA((2, n, pieces)),
         ],
         compiler_params=pltpu.CompilerParams(
-            collective_id=0, has_side_effects=True, vmem_limit_bytes=24 << 20
+            collective_id=0, has_side_effects=True, vmem_limit_bytes=36 << 20
         ),
-    )(frames)
+    )(frames, styles, jnp.transpose(w_qkv, (1, 0, 2)))
 
 
 def scatter_kernel(n, pieces, a_ref, w_ref, out_ref, going, landed, send_sem, recv_sem):
@@ -225,15 +262,10 @@
     chosen = (lax.iota(jnp.int32, n_levels) == levels[0]).astype(jnp.float32)
     styles = jnp.tensordot(chosen, modulation, axes=1, precision=lax.Precision.HIGHEST)
     ranks = lax.axis_size("head")
-    floats = gather_rows(frames, ranks).reshape(1, -1, frames.shape[2]).astype(jnp.float32)
-    normed = floats * lax.rsqrt(jnp.mean(floats * floats, axis=-1, keepdims=True) + 1e-06)
-    shaped = (normed * (1.0 + styles[1]) + styles[0]).astype(jnp.bfloat16)
-    qkv = jnp.einsum("crd,dke->crke", shaped, w_qkv, preferred_element_type=jnp.float32).astype(
-        jnp.bfloat16
-    )
-    total_rows = qkv.shape[1]
-    queries = qkv[0, :, 0].reshape(total_rows, heads_here, HD)
-    kv_block = qkv[:, :, 1:]
+    queries, kv_block = project_rows(frames, styles, w_qkv, ranks)
+    total_rows = queries.shape[0] * queries.shape[1]
+    queries = queries.reshape(total_rows, heads_here, HD)
+    kv_block = kv_block.reshape(1, 2, total_rows, col_width)
     visible_row = visible[0]
     score_scale = HD ** (-0.5)
 
@@ -241,8 +273,8 @@
         row_peak, denominator, running = state
         blocks = incoming.shape[0]
         allowed = (lax.dynamic_slice_in_dim(visible_row, offset, blocks) > 0) & (offset >= 0)
-        key_rows = incoming[:, :, 0].reshape(blocks, total_rows, heads_here, HD)
-        values = incoming[:, :, 1].reshape(blocks, total_rows, heads_here, HD)
+        key_rows = incoming[:, 0].reshape(blocks, total_rows, heads_here, HD)
+        values = incoming[:, 1].reshape(blocks, total_rows, heads_here, HD)
         scores = (
             jnp.einsum("qhd,nkhd->qhnk", queries, key_rows, preferred_element_type=jnp.float32)
             * score_scale

time: 145 us -> 138 us (0.952)
  the two profiles are of different devices: /device:TPU:0 before, /device:TPU:10 now
where the time goes in v2:
time: 138 us; the launch traced here: 137 us
  Pallas kernels  113 us (82%)
  local copies, waits for them, and re-layouts  8.36 us (6%)
  waiting for transfers between devices  4.91 us (4%)
  starting transfers between devices  3.89 us (3%)
  between operations  3.62 us (3%)
  matrix products  2.47 us (2%)
  other arithmetic  1.41 us (1%)
    pallas_call x1, Pallas kernels, scatter_sum(): pl.pallas_call(functools.partial(scatter_kernel, n, pieces), out_shape=ja...  59.6 us
    pallas_call x1, Pallas kernels, project_rows(): pl.pallas_call(functools.partial(project_kernel, n, pieces), out_shape=(j...  53 us
    unnamed x10, local copies, waits for them, and re-layouts  7.06 us
    ppermute x3, waiting for transfers between devices, from_behind(): return lax.ppermute(value, axis, pairs)  4.91 us
    ppermute x3, starting transfers between devices, from_behind(): return lax.ppermute(value, axis, pairs)  3.89 us
  transfers between devices with their start and end apart: 3, of which 2 were waited for; matrix products, arithmetic and copies ran while one was open for 1% of the time, Pallas kernels for 0%

profile of v2, /device:TPU:10, one launch (start us, length us, event | category | flops | bytes accessed | tf_op | source)
XLA Modules:
  0.0 137.3 jit_solution(8599182713760574199)
XLA Ops:
  0.7 0.4 copy-done
  1.1 0.4 fusion.50
  1.5 3.7 %copy-done.1 = bf16[6144,3,256]{2,0,1:T(8,128)(2,1)S(1)} copy-done((bf16[6144,3,256]{2,0,1:T(8,128)(2,1)S(1)}, bf16[6144,3,256]{2,0,1:T(8,128)(2,1)}, u32[]{:S(2)}) %copy-start.1) | copy-done | bytes 9437208
  5.2 1.1 copy-done.3
  6.3 53.0 %shard_map.64 = (bf16[4,64,256]{2,1,0:T(8,128)(2,1)S(1)}, bf16[2,4,64,256]{3,2,1,0:T(8,128)(2,1)S(1)}) custom-call(bf16[1,64,6144]{2,1,0:T(8,128)(2,1)S(1)} %copy-done.3, f32[3,6144]{1,0:T(4,128)S(1)} %bitcast.99, bf16[3,6144,256]{2,1,0:T(8,128)(2,1)S(1)} %bitcast.96), custom_call_target="tpu_custom_call" | custom-call | tf_op jit(solution)/shard_map/pallas_call | solution.py:124
  59.5 1.3 collective-permute-start.1
  60.8 0.7 collective-permute-start.2
  61.5 1.9 %collective-permute-start = (bf16[1,2,256,256]{2,3,1,0:T(8,128)(2,1)S(1)}, bf16[1,2,256,256]{2,3,1,0:T(8,128)(2,1)S(1)}, u32[]{:S(2)}, u32[]{:S(2)}) collective-permute-start(bf16[1,2,256,256]{2,3,1,0:T(8,128)(2,1)S(1)} %copy.20), channel_id=1, source_target_pairs={{0,4},{4,8},{8,12},{1,5},{5,9},{9,13},{2,6},{6,10},{10,14},{3,7},{... | collective-permute-start | bytes 786440 | tf_op jit(solution)/shard_map/ppermute | solution.py:255
  63.5 0.7 constant_dynamic-slice_fusion.2
  64.9 0.3 fusion.68
  67.3 3.3 %collective-permute-done.1 = bf16[1,2,256,256]{2,3,1,0:T(8,128)(2,1)S(1)} collective-permute-done((bf16[1,2,256,256]{2,3,1,0:T(8,128)(2,1)S(1)}, bf16[1,2,256,256]{2,3,1,0:T(8,128)(2,1)S(1)}, u32[]{:S(2)}, u32[]{:S(2)}) %collective-permute-start.1) | collective-permute-done | bytes 262176 | tf_op jit(solution)/shard_map/ppermute | solution.py:255
  70.6 1.6 %collective-permute-done = bf16[1,2,256,256]{2,3,1,0:T(8,128)(2,1)S(1)} collective-permute-done((bf16[1,2,256,256]{2,3,1,0:T(8,128)(2,1)S(1)}, bf16[1,2,256,256]{2,3,1,0:T(8,128)(2,1)S(1)}, u32[]{:S(2)}, u32[]{:S(2)}) %collective-permute-start) | collective-permute-done | bytes 262176 | tf_op jit(solution)/shard_map/ppermute | solution.py:255
  72.2 0.3 fusion.67
  72.5 0.3 fusion.66
  72.9 0.3 fusion.65
  73.2 0.2 fusion.18
  73.4 0.2 fusion.22
  73.6 0.2 fusion.15
  73.8 0.2 fusion.13
  74.1 0.2 fusion.11
  74.3 0.2 fusion.16
  74.8 1.9 %copy-done.2 = bf16[256,6144]{1,0:T(8,128)(2,1)S(1)} copy-done((bf16[256,6144]{1,0:T(8,128)(2,1)S(1)}, bf16[256,6144]{1,0:T(8,128)(2,1)}, u32[]{:S(2)}) %copy-start.2) | copy-done | bytes 3145752
  76.7 59.6 %shard_map.65 = f32[64,6144]{1,0:T(8,128)S(1)} custom-call(bf16[4,64,256]{2,1,0:T(8,128)(2,1)S(1)} %reshape_reshape.3.a_ref, bf16[256,6144]{1,0:T(8,128)(2,1)S(1)} %copy-done.2), custom_call_target="tpu_custom_call" | custom-call | tf_op jit(solution)/shard_map/pallas_call | solution.py:235
  136.3 1.0 fusion.17
  (21 shorter events, 0.7 us)
Async XLA Ops:
  0.0 1.1 copy-start
  1.5 3.7 %copy-start.1 = (bf16[6144,3,256]{2,0,1:T(8,128)(2,1)S(1)}, bf16[6144,3,256]{2,0,1:T(8,128)(2,1)}, u32[]{:S(2)}) copy-start(bf16[6144,3,256]{2,0,1:T(8,128)(2,1)} %param.9) | copy-start | bytes 28311556
  5.2 1.1 copy-start.3
  6.3 57.2 %copy-start.4 = (s32[1,4]{1,0:T(1,128)S(1)}, s32[1,4]{1,0:T(1,128)}, u32[]{:S(2)}) copy-start(s32[1,4]{1,0:T(1,128)} %param.8) | copy-start | bytes 52
  59.5 11.1 %collective-permute-start.1 = (bf16[1,2,256,256]{2,3,1,0:T(8,128)(2,1)S(1)}, bf16[1,2,256,256]{2,3,1,0:T(8,128)(2,1)S(1)}, u32[]{:S(2)}, u32[]{:S(2)}) collective-permute-start(bf16[1,2,256,256]{2,3,1,0:T(8,128)(2,1)S(1)} %copy.20), channel_id=1, source_target_pairs={{0,8},{4,12},{1,9},{5,13},{2,10},{6,14},{3,11},{7,15},{16,24},{20,... | collective-permute-start | bytes 786440 | tf_op jit(solution)/shard_map/ppermute | solution.py:255
  60.8 12.0 %collective-permute-start.2 = (bf16[1,2,256,256]{2,3,1,0:T(8,128)(2,1)S(1)}, bf16[1,2,256,256]{2,3,1,0:T(8,128)(2,1)S(1)}, u32[]{:S(2)}, u32[]{:S(2)}) collective-permute-start(bf16[1,2,256,256]{2,3,1,0:T(8,128)(2,1)S(1)} %copy.20), channel_id=1, source_target_pairs={{0,12},{1,13},{2,14},{3,15},{16,28},{17,29},{18,30},{19,31}} | collective-permute-start | bytes 786440 | tf_op jit(solution)/shard_map/ppermute | solution.py:255
  61.5 10.7 %collective-permute-start = (bf16[1,2,256,256]{2,3,1,0:T(8,128)(2,1)S(1)}, bf16[1,2,256,256]{2,3,1,0:T(8,128)(2,1)S(1)}, u32[]{:S(2)}, u32[]{:S(2)}) collective-permute-start(bf16[1,2,256,256]{2,3,1,0:T(8,128)(2,1)S(1)} %copy.20), channel_id=1, source_target_pairs={{0,4},{4,8},{8,12},{1,5},{5,9},{9,13},{2,6},{6,10},{10,14},{3,7},{... | collective-permute-start | bytes 786440 | tf_op jit(solution)/shard_map/ppermute | solution.py:255
  74.8 1.9 %copy-start.2 = (bf16[256,6144]{1,0:T(8,128)(2,1)S(1)}, bf16[256,6144]{1,0:T(8,128)(2,1)}, u32[]{:S(2)}) copy-start(bf16[256,6144]{1,0:T(8,128)(2,1)} %w_ref.1) | copy-start | bytes 9437188

commit v3 on v2

--- a/solution.py
+++ b/solution.py
@@ -8,6 +8,7 @@
 from jax.sharding import PartitionSpec as P
 
 HD = 128
+GRANT = 60 * 1024 * 1024
 MESH = pl.DeviceIdType.MESH
 
 
@@ -22,7 +23,9 @@
     n, pieces, x_ref, style_ref, w_hbm, q_ref, kv_ref, got, w_ref, w_sem, send_sem, recv_sem
 ):
     me = lax.axis_index("head")
-    load = pltpu.make_async_copy(w_hbm, w_ref, w_sem)
+    own = pltpu.make_async_copy(x_ref.at[0], got.at[me], w_sem.at[0])
+    own.start()
+    load = pltpu.make_async_copy(w_hbm, w_ref, w_sem.at[1])
     load.start()
     meet(n, me)
     rows, width = x_ref.shape[1:]
@@ -81,7 +84,7 @@
             def _():
                 copy(way, 0, piece, True).start()
 
-    got[me] = x_ref[0]
+    own.wait()
     load.wait()
     project(me)
 
@@ -121,30 +124,36 @@
     cols = w_qkv.shape[2]
     pieces = max(1, rows // 32)
     vmem = pl.BlockSpec(memory_space=pltpu.VMEM)
+    hbm = pl.BlockSpec(memory_space=pltpu.HBM)
     return pl.pallas_call(
         functools.partial(project_kernel, n, pieces),
         out_shape=(
             jax.ShapeDtypeStruct((n, rows, cols), frames.dtype),
             jax.ShapeDtypeStruct((2, n, rows, cols), frames.dtype),
         ),
-        in_specs=[vmem, vmem, pl.BlockSpec(memory_space=pl.ANY)],
+        in_specs=[hbm, vmem, hbm],
         out_specs=(vmem, vmem),
         scratch_shapes=[
             pltpu.VMEM((n, rows, width), frames.dtype),
             pltpu.VMEM((3, width, cols), w_qkv.dtype),
-            pltpu.SemaphoreType.DMA,
+            pltpu.SemaphoreType.DMA((2,)),
             pltpu.SemaphoreType.DMA((2, n, pieces)),
             pltpu.SemaphoreType.DMA((2, n, pieces)),
         ],
         compiler_params=pltpu.CompilerParams(
-            collective_id=0, has_side_effects=True, vmem_limit_bytes=36 << 20
+            collective_id=0, has_side_effects=True, vmem_limit_bytes=GRANT
         ),
     )(frames, styles, jnp.transpose(w_qkv, (1, 0, 2)))
 
 
-def scatter_kernel(n, pieces, a_ref, w_ref, out_ref, going, landed, send_sem, recv_sem):
+def scatter_kernel(
+    n, pieces, a_ref, w_hbm, out_ref, w_ref, going, landed, w_sem, send_sem, recv_sem
+):
     me = lax.axis_index("head")
+    load = pltpu.make_async_copy(w_hbm, w_ref, w_sem)
+    load.start()
     meet(n, me)
+    load.wait()
     rows = out_ref.shape[0]
     width = w_ref.shape[1]
     cols = width // pieces
@@ -235,16 +244,21 @@
     return pl.pallas_call(
         functools.partial(scatter_kernel, n, pieces),
         out_shape=jax.ShapeDtypeStruct((rows, width), jnp.float32),
-        in_specs=[pl.BlockSpec(memory_space=pltpu.VMEM)] * 2,
+        in_specs=[
+            pl.BlockSpec(memory_space=pltpu.VMEM),
+            pl.BlockSpec(memory_space=pltpu.HBM),
+        ],
         out_specs=pl.BlockSpec(memory_space=pltpu.VMEM),
         scratch_shapes=[
+            pltpu.VMEM(w_out.shape, w_out.dtype),
             pltpu.VMEM((2, n - 1, rows, width), jnp.bfloat16),
             pltpu.VMEM((2, n - 1, rows, width), jnp.bfloat16),
+            pltpu.SemaphoreType.DMA,
             pltpu.SemaphoreType.DMA((2, n, pieces)),
             pltpu.SemaphoreType.DMA((2, n, pieces)),
         ],
         compiler_params=pltpu.CompilerParams(
-            collective_id=1, has_side_effects=True, vmem_limit_bytes=40 << 20
+            collective_id=1, has_side_effects=True, vmem_limit_bytes=GRANT
         ),
     )(attended.reshape(n, rows, depth), w_out)
 

time: 138 us -> 138 us (level)
  Pallas kernels: 113 us -> 116 us
  local copies, waits for them, and re-layouts: 8.36 us -> 5.78 us
  waiting for transfers between devices: 4.91 us -> 3.22 us
  other arithmetic: 1.41 us -> 2.81 us
    unnamed x10 -> x6, local copies, waits for them, and re-layouts: 7.06 us -> 0.37 us
    pallas_call x1, Pallas kernels: 59.6 us -> 61.7 us  [scatter_sum(): pl.pallas_call(functools.partial(scatter_kernel, n, pieces), out_shape=ja...]
    ppermute x3, waiting for transfers between devices: 4.91 us -> 3.22 us  [from_behind(): return lax.ppermute(value, axis, pairs)]
    broadcast_in_dim x1, other arithmetic: 0.98 us -> 2.39 us  [body(): return mixed[None]]
  transfers between devices with their start and end apart: 3 -> 3, of which waited for: 2 -> 2; matrix products, arithmetic and copies ran while one was open for 1% -> 3% of each run, Pallas kernels for 0% -> 0%
where the time goes in v3:
time: 138 us
  Pallas kernels  116 us (84%)
  local copies, waits for them, and re-layouts  5.78 us (4%)
  starting transfers between devices  3.89 us (3%)
  between operations  3.48 us (3%)
  waiting for transfers between devices  3.22 us (2%)
  other arithmetic  2.81 us (2%)
  matrix products  2.48 us (2%)
    pallas_call x1, Pallas kernels, scatter_sum(): pl.pallas_call(functools.partial(scatter_kernel, n, pieces), out_shape=ja...  61.7 us
    pallas_call x1, Pallas kernels, project_rows(): pl.pallas_call(functools.partial(project_kernel, n, pieces), out_shape=(j...  54.2 us
    ppermute x3, starting transfers between devices, from_behind(): return lax.ppermute(value, axis, pairs)  3.89 us
    ppermute x3, waiting for transfers between devices, from_behind(): return lax.ppermute(value, axis, pairs)  3.22 us
  transfers between devices with their start and end apart: 3, of which 2 were waited for; matrix products, arithmetic and copies ran while one was open for 3% of the time, Pallas kernels for 0%

profile of v3, /device:TPU:10, one launch (start us, length us, event | category | flops | bytes accessed | tf_op | source)
XLA Modules:
  0.0 137.6 jit_solution(11776825651969224775)
XLA Ops:
  0.7 0.4 copy-done
  1.1 0.4 fusion.50
  1.5 0.7 copy.64
  2.2 54.2 %shard_map.64 = (bf16[4,64,256]{2,1,0:T(8,128)(2,1)}, bf16[2,4,64,256]{3,2,1,0:T(8,128)(2,1)}) custom-call(bf16[1,64,6144]{2,1,0:T(8,128)(2,1)} %x_ref.1, f32[3,6144]{1,0:T(4,128)} %bitcast.106, bf16[3,6144,256]{2,1,0:T(8,128)(2,1)} %bitcast.96), custom_call_target="tpu_custom_call" | custom-call | tf_op jit(solution)/shard_map/pallas_call | solution.py:128
  56.4 1.1 copy.20
  57.6 1.3 collective-permute-start.1
  58.9 0.7 collective-permute-start.2
  59.5 1.9 %collective-permute-start = (bf16[1,2,256,256]{2,3,1,0:T(8,128)(2,1)S(1)}, bf16[1,2,256,256]{2,3,1,0:T(8,128)(2,1)S(1)}, u32[]{:S(2)}, u32[]{:S(2)}) collective-permute-start(bf16[1,2,256,256]{2,3,1,0:T(8,128)(2,1)S(1)} %copy.20), channel_id=1, source_target_pairs={{0,4},{4,8},{8,12},{1,5},{5,9},{9,13},{2,6},{6,10},{10,14},{3,7},{... | collective-permute-start | bytes 786440 | tf_op jit(solution)/shard_map/ppermute | solution.py:269
  61.5 0.9 reshape.188
  62.5 0.7 constant_dynamic-slice_fusion.2
  63.8 0.3 fusion.68
  64.1 0.9 slice.44
  67.0 1.6 %collective-permute-done.1 = bf16[1,2,256,256]{2,3,1,0:T(8,128)(2,1)S(1)} collective-permute-done((bf16[1,2,256,256]{2,3,1,0:T(8,128)(2,1)S(1)}, bf16[1,2,256,256]{2,3,1,0:T(8,128)(2,1)S(1)}, u32[]{:S(2)}, u32[]{:S(2)}) %collective-permute-start.1) | collective-permute-done | bytes 262176 | tf_op jit(solution)/shard_map/ppermute | solution.py:269
  68.7 1.6 %collective-permute-done = bf16[1,2,256,256]{2,3,1,0:T(8,128)(2,1)S(1)} collective-permute-done((bf16[1,2,256,256]{2,3,1,0:T(8,128)(2,1)S(1)}, bf16[1,2,256,256]{2,3,1,0:T(8,128)(2,1)S(1)}, u32[]{:S(2)}, u32[]{:S(2)}) %collective-permute-start) | collective-permute-done | bytes 262176 | tf_op jit(solution)/shard_map/ppermute | solution.py:269
  70.3 0.3 fusion.67
  70.6 0.3 fusion.66
  70.9 0.3 fusion.65
  71.6 0.2 fusion.15
  71.9 0.2 fusion.13
  72.1 0.2 fusion.11
  72.4 0.2 fusion.16
  72.7 0.7 reshape_reshape.3.a_ref
  73.5 61.7 %shard_map.65 = f32[64,6144]{1,0:T(8,128)} custom-call(bf16[4,64,256]{2,1,0:T(8,128)(2,1)} %reshape_reshape.3.a_ref, bf16[256,6144]{1,0:T(8,128)(2,1)} %w_hbm.1), custom_call_target="tpu_custom_call" | custom-call | tf_op jit(solution)/shard_map/pallas_call | solution.py:244
  135.2 2.4 %fusion.17 = bf16[1,64,6144]{2,1,0:T(8,128)(2,1)} fusion(f32[64,6144]{1,0:T(8,128)} %shard_map.65, f32[6144]{0:T(1024)S(1)} %bitcast.109), kind=kLoop, calls=%fused_computation.26 | loop fusion | flops 786432 | bytes 2383872 | tf_op jit(solution)/shard_map/broadcast_in_dim | solution.py:324
  (17 shorter events, 0.7 us)
Async XLA Ops:
  0.0 1.1 copy-start
  2.2 60.3 %copy-start.2 = (s32[1,4]{1,0:T(1,128)S(1)}, s32[1,4]{1,0:T(1,128)}, u32[]{:S(2)}) copy-start(s32[1,4]{1,0:T(1,128)} %param.8) | copy-start | bytes 52
  56.4 8.6 %copy-start.1 = (bf16[2,4,64,256]{3,2,1,0:T(8,128)(2,1)S(1)}, bf16[2,4,64,256]{3,2,1,0:T(8,128)(2,1)}, u32[]{:S(2)}) copy-start(bf16[2,4,64,256]{3,2,1,0:T(8,128)(2,1)} %get-tuple-element.7) | copy-start | bytes 786436
  57.6 11.1 %collective-permute-start.1 = (bf16[1,2,256,256]{2,3,1,0:T(8,128)(2,1)S(1)}, bf16[1,2,256,256]{2,3,1,0:T(8,128)(2,1)S(1)}, u32[]{:S(2)}, u32[]{:S(2)}) collective-permute-start(bf16[1,2,256,256]{2,3,1,0:T(8,128)(2,1)S(1)} %copy.20), channel_id=1, source_target_pairs={{0,8},{4,12},{1,9},{5,13},{2,10},{6,14},{3,11},{7,15},{16,24},{20,... | collective-permute-start | bytes 786440 | tf_op jit(solution)/shard_map/ppermute | solution.py:269
  58.9 12.0 %collective-permute-start.2 = (bf16[1,2,256,256]{2,3,1,0:T(8,128)(2,1)S(1)}, bf16[1,2,256,256]{2,3,1,0:T(8,128)(2,1)S(1)}, u32[]{:S(2)}, u32[]{:S(2)}) collective-permute-start(bf16[1,2,256,256]{2,3,1,0:T(8,128)(2,1)S(1)} %copy.20), channel_id=1, source_target_pairs={{0,12},{1,13},{2,14},{3,15},{16,28},{17,29},{18,30},{19,31}} | collective-permute-start | bytes 786440 | tf_op jit(solution)/shard_map/ppermute | solution.py:269
  59.5 10.7 %collective-permute-start = (bf16[1,2,256,256]{2,3,1,0:T(8,128)(2,1)S(1)}, bf16[1,2,256,256]{2,3,1,0:T(8,128)(2,1)S(1)}, u32[]{:S(2)}, u32[]{:S(2)}) collective-permute-start(bf16[1,2,256,256]{2,3,1,0:T(8,128)(2,1)S(1)} %copy.20), channel_id=1, source_target_pairs={{0,4},{4,8},{8,12},{1,5},{5,9},{9,13},{2,6},{6,10},{10,14},{3,7},{... | collective-permute-start | bytes 786440 | tf_op jit(solution)/shard_map/ppermute | solution.py:269

commit v4 on v2

v4 whole, which is shorter than its diff:
```python
import functools

import jax
import jax.numpy as jnp
from jax import lax
from jax.experimental import pallas as pl
from jax.experimental.pallas import tpu as pltpu
from jax.sharding import PartitionSpec as P

HD = 128
GRANT = 60 * 1024 * 1024
MESH = pl.DeviceIdType.MESH


def meet(n, me, tracts, tract):
    barrier = pltpu.get_barrier_semaphore()
    for other in (lax.rem(me + 1, n), lax.rem(me + n - 1, n)):
        pl.semaphore_signal(barrier, inc=1, device_id={"head": other}, device_id_type=MESH)
    for ahead in range(1, tracts):
        other = lax.rem(tract + ahead, tracts)
        pl.semaphore_signal(barrier, inc=1, device_id={"tract": other}, device_id_type=MESH)
    pl.semaphore_wait(barrier, 1 + tracts)


def sublayer_kernel(
    n,
    tracts,
    pieces,
    halves,
    x_ref,
    level_ref,
    visible_ref,
    w_hbm,
    out_hbm,
    table_ref,
    out_ref,
    got,
    wq_ref,
    w_ref,
    q_ref,
    kv_ref,
    kv_in,
    att_ref,
    peak_ref,
    sum_ref,
    acc_ref,
    going,
    landed,
    total_ref,
    load_sem,
    g_send,
    g_recv,
    kv_send,
    kv_recv,
    s_send,
    s_recv,
):
    me, tract = lax.axis_index("head"), lax.axis_index("tract")
    own = pltpu.make_async_copy(x_ref.at[0], got.at[me], load_sem.at[0])
    own.start()
    load = pltpu.make_async_copy(w_hbm, wq_ref, load_sem.at[1])
    load.start()
    load_out = pltpu.make_async_copy(out_hbm, w_ref, load_sem.at[2])
    load_out.start()
    meet(n, me, tracts, tract)
    level = level_ref[0]

    def style(kind):
        return table_ref[kind, pl.ds(level, 1), :]

    rows, width = x_ref.shape[1:]
    part = rows // pieces

    def copy(way, step, piece, first=False):
        side = (way + 1) // 2
        span = pl.ds(piece * part, part)
        block = me - way * step
        return pltpu.make_async_remote_copy(
            src_ref=(x_ref.at[0] if first else got.at[block]).at[span],
            dst_ref=got.at[block].at[span],
            send_sem=g_send.at[side, step, piece],
            recv_sem=g_recv.at[side, step, piece],
            device_id={"head": me + way},
            device_id_type=MESH,
        )

    def arrival(way, step, piece):
        side = (way + 1) // 2
        span = pl.ds(piece * part, part)
        return pltpu.make_async_remote_copy(
            src_ref=x_ref.at[0].at[span],
            dst_ref=got.at[me - way * (step + 1)].at[span],
            send_sem=g_send.at[side, step, piece],
            recv_sem=g_recv.at[side, step, piece],
            device_id={"head": me - way},
            device_id_type=MESH,
        )

    def sends(way, step):
        block, target = me - way * step, me + way
        return (block >= 0) & (block < n) & (target >= 0) & (target < n) & (step < n - 1)

    def receives(way, step):
        block = me - way * (step + 1)
        return (block >= 0) & (block < n)

    def kv_copy(ahead, block):
        return pltpu.make_async_remote_copy(
            src_ref=kv_ref.at[block],
            dst_ref=kv_in.at[ahead - 1, block],
            send_sem=kv_send.at[ahead - 1, block],
            recv_sem=kv_recv.at[ahead - 1, block],
            device_id={"tract": tract + ahead},
            device_id_type=MESH,
        )

    def project(block):
        tokens = got[block].astype(jnp.float32)
        power = jnp.mean(tokens * tokens, axis=-1, keepdims=True)
        normed = tokens * lax.rsqrt(power + 1e-06)
        shaped = (normed * (1.0 + style(1)) + style(0)).astype(jnp.bfloat16)
        for kind in (1, 2, 0):
            made = jnp.dot(shaped, wq_ref[kind], preferred_element_type=jnp.float32)
            made = made.astype(jnp.bfloat16)
            if kind == 0:
                q_ref[block] = made
            else:
                kv_ref[block, kind - 1] = made
            if kind == 2:
                for ahead in range(1, tracts):

                    @pl.when(tract + ahead < tracts)
                    def _():
                        kv_copy(ahead, block).start()

    for piece in range(pieces):
        for way in (-1, 1):

            @pl.when(sends(way, 0))
            def _():
                copy(way, 0, piece, True).start()

    own.wait()
    load.wait()
    project(me)

    @pl.loop(0, n - 1)
    def _(step):
        for piece in range(pieces):
            for way in (-1, 1):

                @pl.when(receives(way, step))
                def _():
                    arrival(way, step, piece).wait_recv()

                @pl.when(sends(way, step + 1))
                def _():
                    copy(way, step + 1, piece).start()

        @pl.loop(0, 2)
        def _(side):
            way = 2 * side - 1

            @pl.when(receives(way, step))
            def _():
                project(me - way * (step + 1))

    @pl.loop(0, n - 1)
    def _(step):
        for piece in range(pieces):
            for way in (-1, 1):

                @pl.when(sends(way, step))
                def _():
                    copy(way, step, piece).wait_send()

    tokens_here = n * rows
    heads_here = q_ref.shape[2] // HD
    scale = HD ** (-0.5)

    def attend(source, allowed):
        for head in range(heads_here):
            lanes = slice(head * HD, (head + 1) * HD)
            queries = q_ref[:, :, lanes].reshape(tokens_here, HD)
            keys = source[:, 0, :, lanes].reshape(tokens_here, HD)
            values = source[:, 1, :, lanes].reshape(tokens_here, HD)
            scores = (
                lax.dot_general(
                    queries, keys, (((1,), (1,)), ((), ())), preferred_element_type=jnp.float32
                )
                * scale
            )
            if allowed is None:
                peak = jnp.max(scores, axis=1, keepdims=True)
                probs = jnp.exp(scores - peak)
            else:
                scores = jnp.where(allowed, scores, -1e30)
                old = peak_ref[head]
                peak = jnp.maximum(old, jnp.max(scores, axis=1, keepdims=True))
                probs = jnp.where(allowed, jnp.exp(scores - peak), 0.0)
                rescale = jnp.exp(old - peak)
            row_sum = jnp.sum(probs, axis=1, keepdims=True)
            weighted = jnp.dot(
                probs.astype(jnp.bfloat16), values, preferred_element_type=jnp.float32
            )
            if allowed is not None:
                row_sum += sum_ref[head] * rescale
                weighted += acc_ref[head] * rescale
            peak_ref[head] = peak
            sum_ref[head] = row_sum
            acc_ref[head] = weighted

    attend(kv_ref, None)
    for ahead in range(1, tracts):

        @pl.when(tract >= ahead)
        def _():
            @pl.loop(0, n)
            def _(block):
                kv_copy(ahead, block).wait_recv()

            attend(kv_in.at[ahead - 1], visible_ref[0, lax.max(tract - ahead, 0)] > 0)

    for head in range(heads_here):
        attended = (acc_ref[head] / sum_ref[head]).astype(jnp.bfloat16)
        att_ref[:, :, head * HD : (head + 1) * HD] = attended.reshape(n, rows, HD)
    load_out.wait()
    cols = width // halves

    def sum_copy(way, step, piece):
        side = (way + 1) // 2
        span = pl.ds(piece * cols, cols)
        return pltpu.make_async_remote_copy(
            src_ref=going.at[side, step].at[:, span],
            dst_ref=landed.at[side, step].at[:, span],
            send_sem=s_send.at[side, step, piece],
            recv_sem=s_recv.at[side, step, piece],
            device_id={"head": me + way},
            device_id_type=MESH,
        )

    def product(block, piece):
        return jnp.dot(
            att_ref[block],
            w_ref[:, piece * cols : (piece + 1) * cols],
            preferred_element_type=jnp.float32,
        )

    def owner(way, step):
        return (n - 1 - step) if way == 1 else step

    def sum_sends(way, step):
        block = owner(way, step)
        return block > me if way == 1 else block < me

    def sum_receives(way, step):
        block = owner(way, step)
        return (block >= me) & (me > 0) if way == 1 else (block <= me) & (me < n - 1)

    @pl.loop(0, n - 1)
    def _(tick):
        for piece in range(halves):
            span = slice(piece * cols, (piece + 1) * cols)
            for way in (-1, 1):
                side = (way + 1) // 2
                step = tick - (me if way == 1 else n - 1 - me)
                held = (step >= 0) & (step < n - 1)

                @pl.when(held & sum_sends(way, step))
                def _():
                    going[side, step, :, span] = product(owner(way, step), piece).astype(
                        going.dtype
                    )

                    @pl.when(sum_receives(way, step))
                    def _():
                        sum_copy(way, step, piece).wait_recv()
                        going[side, step, :, span] = (
                            going[side, step, :, span].astype(jnp.float32)
                            + landed[side, step, :, span].astype(jnp.float32)
                        ).astype(going.dtype)

                    sum_copy(way, step, piece).start()

    for piece in range(halves):
        span = slice(piece * cols, (piece + 1) * cols)
        total_ref[:, span] = product(me, piece).astype(going.dtype).astype(jnp.float32)
    for piece in range(halves):
        span = slice(piece * cols, (piece + 1) * cols)
        for way in (-1, 1):
            side = (way + 1) // 2
            last = n - 1 - me if way == 1 else me

            @pl.when(last < n - 1)
            def _():
                sum_copy(way, last, piece).wait_recv()
                total_ref[:, span] += landed[side, last, :, span].astype(jnp.float32)

        out_ref[0, :, span] = (
            total_ref[:, span] * table_ref[2, pl.ds(level, 1), span]
        ).astype(out_ref.dtype)

    @pl.loop(0, n - 1)
    def _(step):
        for piece in range(halves):
            for way in (-1, 1):

                @pl.when(sum_sends(way, step))
                def _():
                    sum_copy(way, step, piece).wait_send()

    @pl.loop(0, n)
    def _(block):
        for ahead in range(1, tracts):

            @pl.when(tract + ahead < tracts)
            def _():
                kv_copy(ahead, block).wait_send()


def body(frames, levels, visible, w_qkv, w_out, modulation):
    n, tracts = lax.axis_size("head"), lax.axis_size("tract")
    rows, width = frames.shape[1:]
    cols = w_qkv.shape[2]
    heads_here = cols // HD
    pieces = max(1, rows // 32)
    halves = 2
    vmem = pl.BlockSpec(memory_space=pltpu.VMEM)
    hbm = pl.BlockSpec(memory_space=pltpu.HBM)
    smem = pl.BlockSpec(memory_space=pltpu.SMEM)
    half = jnp.bfloat16
    dma = pltpu.SemaphoreType.DMA
    return pl.pallas_call(
        functools.partial(sublayer_kernel, n, tracts, pieces, halves),
        out_shape=jax.ShapeDtypeStruct(frames.shape, frames.dtype),
        in_specs=[hbm, smem, smem, hbm, hbm, vmem],
        out_specs=vmem,
        scratch_shapes=[
            pltpu.VMEM((n, rows, width), half),
            pltpu.VMEM((3, width, cols), half),
            pltpu.VMEM(w_out.shape, half),
            pltpu.VMEM((n, rows, cols), half),
            pltpu.VMEM((n, 2, rows, cols), half),
            pltpu.VMEM((max(1, tracts - 1), n, 2, rows, cols), half),
            pltpu.VMEM((n, rows, cols), half),
            pltpu.VMEM((heads_here, n * rows, 1), jnp.float32),
            pltpu.VMEM((heads_here, n * rows, 1), jnp.float32),
            pltpu.VMEM((heads_here, n * rows, HD), jnp.float32),
            pltpu.VMEM((2, n - 1, rows, width), half),
            pltpu.VMEM((2, n - 1, rows, width), half),
            pltpu.VMEM((rows, width), jnp.float32),
            dma((3,)),
            dma((2, n, pieces)),
            dma((2, n, pieces)),
            dma((tracts, n)),
            dma((tracts, n)),
            dma((2, n, halves)),
            dma((2, n, halves)),
        ],
        compiler_params=pltpu.CompilerParams(
            collective_id=0, has_side_effects=True, vmem_limit_bytes=GRANT
        ),
    )(
        frames,
        levels,
        visible,
        jnp.transpose(w_qkv, (1, 0, 2)),
        w_out,
        jnp.transpose(modulation, (1, 0, 2)),
    )


def solution(mesh):
    placed = (
        P(("rep", "tract"), "head", None),
        P(("rep", "tract")),
        P(("rep", "tract"), None),
        P(None, None, "head"),
        P("head", None),
        P(),
    )
    return jax.shard_map(
        body,
        mesh=mesh,
        in_specs=placed,
        out_specs=P(("rep", "tract"), "head", None),
        check_vma=False,
    )
```

time: 138 us -> 120 us (0.87)
  local copies, waits for them, and re-layouts: 8.36 us -> 2.06 us
  waiting for transfers between devices: 4.91 us -> 0 us
  Pallas kernels: 113 us -> 117 us
  starting transfers between devices: 3.89 us -> 0 us
  between operations: 3.62 us -> 0.66 us
  matrix products: 2.47 us -> 0 us
  other arithmetic: 1.41 us -> 0 us
    unnamed x10 -> x1, local copies, waits for them, and re-layouts: 7.06 us -> 2.06 us
    ppermute x3 -> x0, waiting for transfers between devices: 4.91 us -> none  [from_behind(): return lax.ppermute(value, axis, pairs)]
    pallas_call x2 -> x1, Pallas kernels: 113 us -> 117 us  [body(): pl.pallas_call(functools.partial(sublayer_kernel, n, tracts, pieces, halv...]
    ppermute x3 -> x0, starting transfers between devices: 3.89 us -> none  [from_behind(): return lax.ppermute(value, axis, pairs)]
    dot_general x9 -> x0, matrix products: 2.47 us -> none  [the longest x4 1.14 us: absorb(): jnp.einsum('qhd,nkhd->qhnk', queries, key_rows, preferred_element_type=jn...]
  transfers between devices with their start and end apart: 3 -> 0, of which waited for: 2 -> 0; matrix products, arithmetic and copies ran while one was open for 1% -> 0% of each run, Pallas kernels for 0% -> 0%
where the time goes in v4:
time: 120 us; the launch traced here: 119 us
  Pallas kernels  117 us (98%)
  local copies, waits for them, and re-layouts  2.06 us (2%)
    pallas_call x1, Pallas kernels, body(): pl.pallas_call(functools.partial(sublayer_kernel, n, tracts, pieces, halv...  117 us

profile of v4, /device:TPU:10, one launch (start us, length us, event | category | flops | bytes accessed | tf_op | source)
XLA Modules:
  0.0 119.3 jit_solution(12178555149483929753)
XLA Ops:
  0.7 116.5 %shard_map.64 = bf16[1,64,6144]{2,1,0:T(8,128)(2,1)} custom-call(bf16[1,64,6144]{2,1,0:T(8,128)(2,1)} %x_ref.1, s32[1]{0:T(128)S(6)} %copy.8.level_ref, s32[1,4]{1,0:T(1,128)} %visible_ref.1, bf16[3,6144,256]{2,1,0:T(8,128)(2,1)} %bitcast.2, bf16[256,6144]{1,0:T(8,128)(2,1)} %out_hbm.1, f32[3,8,6144]{2,1,0:T(8,128)} %bitcast.3), custom_call_target="tpu_custom_call" | custom-call | tf_op jit(solution)/shard_map/pallas_call | solution.py:333
  117.2 2.1 %copy.9 = bf16[1,64,6144]{2,1,0:T(8,128)(2,1)} copy(bf16[1,64,6144]{2,1,0:T(8,128)(2,1)} %shard_map.64) | data formatting | bytes 1572864

commit v5 on v4

--- a/solution.py
+++ b/solution.py
@@ -12,19 +12,22 @@
 MESH = pl.DeviceIdType.MESH
 
 
-def meet(n, me, tracts, tract):
+def meet(n, me, tracts, tract, others):
     barrier = pltpu.get_barrier_semaphore()
     for other in (lax.rem(me + 1, n), lax.rem(me + n - 1, n)):
         pl.semaphore_signal(barrier, inc=1, device_id={"head": other}, device_id_type=MESH)
     for ahead in range(1, tracts):
         other = lax.rem(tract + ahead, tracts)
         pl.semaphore_signal(barrier, inc=1, device_id={"tract": other}, device_id_type=MESH)
-    pl.semaphore_wait(barrier, 1 + tracts)
+    for other in others:
+        pl.semaphore_signal(barrier, inc=1, device_id=other, device_id_type=MESH)
+    pl.semaphore_wait(barrier, 1 + tracts + len(others))
 
 
 def sublayer_kernel(
     n,
     tracts,
+    reps,
     pieces,
     halves,
     x_ref,
@@ -54,6 +57,10 @@
     kv_recv,
     s_send,
     s_recv,
+    w_far,
+    att_far,
+    f_send,
+    f_recv,
 ):
     me, tract = lax.axis_index("head"), lax.axis_index("tract")
     own = pltpu.make_async_copy(x_ref.at[0], got.at[me], load_sem.at[0])
@@ -62,7 +69,63 @@
     load.start()
     load_out = pltpu.make_async_copy(out_hbm, w_ref, load_sem.at[2])
     load_out.start()
-    meet(n, me, tracts, tract)
+    core, wide = tract % 2, tracts // 2
+    chips = wide * reps
+    chip = lax.axis_index("rep") * wide + tract // 2
+    slab = w_ref.shape[0] // (2 * chips)
+    helper = (me == 1) | (me == n - 2)
+    ends = (me == 0) | (me == n - 1)
+
+    def seat(by):
+        other = lax.rem(chip + by, chips)
+        return {"rep": other // wide, "tract": lax.rem(other, wide) * 2 + core}
+
+    def slab_of(which, side):
+        start = pl.multiple_of((which * 2 + side) * slab, slab)
+        return pl.ds(start, slab)
+
+    def far_copy(kind, span, target, source=None):
+        return pltpu.make_async_remote_copy(
+            src_ref=(w_far if source is None else source).at[span],
+            dst_ref=w_far.at[span],
+            send_sem=f_send.at[kind],
+            recv_sem=f_recv.at[kind],
+            device_id=target,
+            device_id_type=MESH,
+        )
+
+    inward = {"head": jnp.where(me == 0, 1, n - 2)}
+    partner = {"tract": tract + 1 - 2 * core}
+    mine = slab_of(chip, core)
+
+    def to_helper():
+        return far_copy(0, mine, inward, out_hbm)
+
+    def to_chip(by):
+        return far_copy(by, mine, seat(by))
+
+    def from_chip(by):
+        return far_copy(by, slab_of(lax.rem(chip + chips - by, chips), core), seat(by))
+
+    def to_partner(by):
+        span = slab_of(lax.rem(chip + chips - by, chips), core)
+        return far_copy(chips + by, span, partner)
+
+    def from_partner(by):
+        span = slab_of(lax.rem(chip + chips - by, chips), 1 - core)
+        return far_copy(chips + by, span, partner)
+
+    def att_copy():
+        return pltpu.make_async_remote_copy(
+            src_ref=att_ref,
+            dst_ref=att_far,
+            send_sem=f_send.at[2 * chips],
+            recv_sem=f_recv.at[2 * chips],
+            device_id=inward,
+            device_id_type=MESH,
+        )
+
+    meet(n, me, tracts, tract, [seat(by) for by in range(1, chips)])
     level = level_ref[0]
 
     def style(kind):
@@ -140,6 +203,10 @@
             def _():
                 copy(way, 0, piece, True).start()
 
+    @pl.when(ends)
+    def _():
+        to_helper().start()
+
     own.wait()
     load.wait()
     project(me)
@@ -164,6 +231,19 @@
             @pl.when(receives(way, step))
             def _():
                 project(me - way * (step + 1))
+
+        @pl.when(helper & (step == 0))
+        def _():
+            to_helper().wait_recv()
+            for by in range(1, chips):
+                to_chip(by).start()
+            to_partner(0).start()
+
+    @pl.when(helper)
+    def _():
+        for by in range(1, chips):
+            from_chip(by).wait_recv()
+            to_partner(by).start()
 
     @pl.loop(0, n - 1)
     def _(step):
@@ -224,7 +304,19 @@
     for head in range(heads_here):
         attended = (acc_ref[head] / sum_ref[head]).astype(jnp.bfloat16)
         att_ref[:, :, head * HD : (head + 1) * HD] = attended.reshape(n, rows, HD)
+
+    @pl.when(ends)
+    def _():
+        att_copy().start()
+
     load_out.wait()
+
+    @pl.when(helper)
+    def _():
+        for by in range(chips):
+            from_partner(by).wait_recv()
+        att_copy().wait_recv()
+
     cols = width // halves
 
     def sum_copy(way, step, piece):
@@ -246,16 +338,26 @@
             preferred_element_type=jnp.float32,
         )
 
+    def far_product(block, piece):
+        return jnp.dot(
+            att_far[block],
+            w_far[:, piece * cols : (piece + 1) * cols],
+            preferred_element_type=jnp.float32,
+        )
+
+    def helps(way):
+        return me == (1 if way == 1 else n - 2)
+
     def owner(way, step):
         return (n - 1 - step) if way == 1 else step
 
     def sum_sends(way, step):
         block = owner(way, step)
-        return block > me if way == 1 else block < me
+        return (block > me) & (me > 0) if way == 1 else (block < me) & (me < n - 1)
 
     def sum_receives(way, step):
         block = owner(way, step)
-        return (block >= me) & (me > 0) if way == 1 else (block <= me) & (me < n - 1)
+        return (block >= me) & (me > 1) if way == 1 else (block <= me) & (me < n - 2)
 
     @pl.loop(0, n - 1)
     def _(tick):
@@ -272,6 +374,13 @@
                         going.dtype
                     )
 
+                    @pl.when(helps(way))
+                    def _():
+                        going[side, step, :, span] = (
+                            going[side, step, :, span].astype(jnp.float32)
+                            + far_product(owner(way, step), piece)
+                        ).astype(going.dtype)
+
                     @pl.when(sum_receives(way, step))
                     def _():
                         sum_copy(way, step, piece).wait_recv()
@@ -291,7 +400,11 @@
             side = (way + 1) // 2
             last = n - 1 - me if way == 1 else me
 
-            @pl.when(last < n - 1)
+            @pl.when(helps(way))
+            def _():
+                total_ref[:, span] += far_product(me, piece)
+
+            @pl.when(me > 1 if way == 1 else me < n - 2)
             def _():
                 sum_copy(way, last, piece).wait_recv()
                 total_ref[:, span] += landed[side, last, :, span].astype(jnp.float32)
@@ -317,9 +430,22 @@
             def _():
                 kv_copy(ahead, block).wait_send()
 
+    @pl.when(ends)
+    def _():
+        to_helper().wait_send()
+        att_copy().wait_send()
+
+    @pl.when(helper)
+    def _():
+        for by in range(1, chips):
+            to_chip(by).wait_send()
+        for by in range(chips):
+            to_partner(by).wait_send()
+
 
 def body(frames, levels, visible, w_qkv, w_out, modulation):
     n, tracts = lax.axis_size("head"), lax.axis_size("tract")
+    reps = lax.axis_size("rep")
     rows, width = frames.shape[1:]
     cols = w_qkv.shape[2]
     heads_here = cols // HD
@@ -331,7 +457,7 @@
     half = jnp.bfloat16
     dma = pltpu.SemaphoreType.DMA
     return pl.pallas_call(
-        functools.partial(sublayer_kernel, n, tracts, pieces, halves),
+        functools.partial(sublayer_kernel, n, tracts, reps, pieces, halves),
         out_shape=jax.ShapeDtypeStruct(frames.shape, frames.dtype),
         in_specs=[hbm, smem, smem, hbm, hbm, vmem],
         out_specs=vmem,
@@ -356,6 +482,10 @@
             dma((tracts, n)),
             dma((2, n, halves)),
             dma((2, n, halves)),
+            pltpu.VMEM(w_out.shape, half),
+            pltpu.VMEM((n, rows, cols), half),
+            dma((tracts * reps + 1,)),
+            dma((tracts * reps + 1,)),
         ],
         compiler_params=pltpu.CompilerParams(
             collective_id=0, has_side_effects=True, vmem_limit_bytes=GRANT

time: 120 us -> 109 us (0.908)
  Pallas kernels: 117 us -> 106 us
    pallas_call x1, Pallas kernels: 117 us -> 106 us  [body(): pl.pallas_call(functools.partial(sublayer_kernel, n, tracts, reps, pieces...]
where the time goes in v5:
time: 109 us
  Pallas kernels  106 us (97%)
  local copies, waits for them, and re-layouts  2.06 us (2%)
    pallas_call x1, Pallas kernels, body(): pl.pallas_call(functools.partial(sublayer_kernel, n, tracts, reps, pieces...  106 us

profile of v5, /device:TPU:10, one launch (start us, length us, event | category | flops | bytes accessed | tf_op | source)
XLA Modules:
  0.0 108.8 jit_solution(12773593515689705686)
XLA Ops:
  0.7 106.1 %shard_map.64 = bf16[1,64,6144]{2,1,0:T(8,128)(2,1)} custom-call(bf16[1,64,6144]{2,1,0:T(8,128)(2,1)} %x_ref.1, s32[1]{0:T(128)S(6)} %copy.8.level_ref, s32[1,4]{1,0:T(1,128)} %visible_ref.1, bf16[3,6144,256]{2,1,0:T(8,128)(2,1)} %bitcast.2, bf16[256,6144]{1,0:T(8,128)(2,1)} %out_hbm.1, f32[3,8,6144]{2,1,0:T(8,128)} %bitcast.3), custom_call_target="tpu_custom_call" | custom-call | tf_op jit(solution)/shard_map/pallas_call | solution.py:459
  106.7 2.1 %copy.9 = bf16[1,64,6144]{2,1,0:T(8,128)(2,1)} copy(bf16[1,64,6144]{2,1,0:T(8,128)(2,1)} %shard_map.64) | data formatting | bytes 1572864

commit v6 on v5

--- a/solution.py
+++ b/solution.py
@@ -245,15 +245,6 @@
             from_chip(by).wait_recv()
             to_partner(by).start()
 
-    @pl.loop(0, n - 1)
-    def _(step):
-        for piece in range(pieces):
-            for way in (-1, 1):
-
-                @pl.when(sends(way, step))
-                def _():
-                    copy(way, step, piece).wait_send()
-
     tokens_here = n * rows
     heads_here = q_ref.shape[2] // HD
     scale = HD ** (-0.5)
@@ -430,6 +421,15 @@
             def _():
                 kv_copy(ahead, block).wait_send()
 
+    @pl.loop(0, n - 1)
+    def _(step):
+        for piece in range(pieces):
+            for way in (-1, 1):
+
+                @pl.when(sends(way, step))
+                def _():
+                    copy(way, step, piece).wait_send()
+
     @pl.when(ends)
     def _():
         to_helper().wait_send()
@@ -450,7 +450,7 @@
     cols = w_qkv.shape[2]
     heads_here = cols // HD
     pieces = max(1, rows // 32)
-    halves = 2
+    halves = 4 if width % 512 == 0 else 2
     vmem = pl.BlockSpec(memory_space=pltpu.VMEM)
     hbm = pl.BlockSpec(memory_space=pltpu.HBM)
     smem = pl.BlockSpec(memory_space=pltpu.SMEM)

time: 109 us -> 109 us (level)
  no operation moved by 1% of the time
where the time goes in v6:
time: 109 us
  Pallas kernels  106 us (97%)
  local copies, waits for them, and re-layouts  2.06 us (2%)
    pallas_call x1, Pallas kernels, body(): pl.pallas_call(functools.partial(sublayer_kernel, n, tracts, reps, pieces...  106 us

profile of v6, /device:TPU:10, one launch (start us, length us, event | category | flops | bytes accessed | tf_op | source)
XLA Modules:
  0.0 108.7 jit_solution(1362124493470144185)
XLA Ops:
  0.7 106.0 %shard_map.64 = bf16[1,64,6144]{2,1,0:T(8,128)(2,1)} custom-call(bf16[1,64,6144]{2,1,0:T(8,128)(2,1)} %x_ref.1, s32[1]{0:T(128)S(6)} %copy.8.level_ref, s32[1,4]{1,0:T(1,128)} %visible_ref.1, bf16[3,6144,256]{2,1,0:T(8,128)(2,1)} %bitcast.2, bf16[256,6144]{1,0:T(8,128)(2,1)} %out_hbm.1, f32[3,8,6144]{2,1,0:T(8,128)} %bitcast.3), custom_call_target="tpu_custom_call" | custom-call | tf_op jit(solution)/shard_map/pallas_call | solution.py:459
  106.6 2.1 %copy.9 = bf16[1,64,6144]{2,1,0:T(8,128)(2,1)} copy(bf16[1,64,6144]{2,1,0:T(8,128)(2,1)} %shard_map.64) | data formatting | bytes 1572864

commit v7 on v6

--- a/solution.py
+++ b/solution.py
@@ -449,7 +449,7 @@
     rows, width = frames.shape[1:]
     cols = w_qkv.shape[2]
     heads_here = cols // HD
-    pieces = max(1, rows // 32)
+    pieces = max(1, rows // 16)
     halves = 4 if width % 512 == 0 else 2
     vmem = pl.BlockSpec(memory_space=pltpu.VMEM)
     hbm = pl.BlockSpec(memory_space=pltpu.HBM)

time: 109 us -> 109 us (level)
  no operation moved by 1% of the time
where the time goes in v7:
time: 109 us
  Pallas kernels  106 us (97%)
  local copies, waits for them, and re-layouts  2.06 us (2%)
    pallas_call x1, Pallas kernels, body(): pl.pallas_call(functools.partial(sublayer_kernel, n, tracts, reps, pieces...  106 us

profile of v7, /device:TPU:10, one launch (start us, length us, event | category | flops | bytes accessed | tf_op | source)
XLA Modules:
  0.0 109.0 jit_solution(5835230877919408084)
XLA Ops:
  0.7 106.3 %shard_map.64 = bf16[1,64,6144]{2,1,0:T(8,128)(2,1)} custom-call(bf16[1,64,6144]{2,1,0:T(8,128)(2,1)} %x_ref.1, s32[1]{0:T(128)S(6)} %copy.8.level_ref, s32[1,4]{1,0:T(1,128)} %visible_ref.1, bf16[3,6144,256]{2,1,0:T(8,128)(2,1)} %bitcast.2, bf16[256,6144]{1,0:T(8,128)(2,1)} %out_hbm.1, f32[3,8,6144]{2,1,0:T(8,128)} %bitcast.3), custom_call_target="tpu_custom_call" | custom-call | tf_op jit(solution)/shard_map/pallas_call | solution.py:459
  106.9 2.1 %copy.9 = bf16[1,64,6144]{2,1,0:T(8,128)(2,1)} copy(bf16[1,64,6144]{2,1,0:T(8,128)(2,1)} %shard_map.64) | data formatting | bytes 1572864
